TPU v7x, 32 devices: a whole 2x2x4 slice. The times are simulated.
32 devices in a mesh: blk: 16 (over z, x, core), tp: 2 (over y).
Axes of the slice: x: 2, y: 2, z: 4, core: 2. Of those that a mesh axis runs over, the one named last changes fastest.
Arguments:
- inputs: bfloat16 [2048, 8192], P('blk', 'tp'), may hold values from -6 to 6
- grad_out: bfloat16 [2048, 8192], P('blk', 'tp'), may hold values from -6 to 6
- w_up: bfloat16 [32, 2, 128, 128], P('blk'), may hold values from -0.4375 to 0.4375
- w_down: bfloat16 [32, 2, 128, 128], P('blk'), may hold values from -0.625 to 0.625
- up_rows: int32 [32, 2], P('blk'), may hold values from 0 to 63, as said below
- slot_counts: int32 [32], P('blk'), may hold values from 1 to 2
- keep_mask: int32 [2048, 256], P(None, 'blk'), may hold values from 0 to 65535, as said below
Outputs:
- outputs: bfloat16 [2048, 8192], P('blk', 'tp')
- grad_in: bfloat16 [2048, 8192], P('blk', 'tp')
- grad_up: bfloat16 [32, 2, 128, 128], P('blk', None, 'tp')
- grad_down: bfloat16 [32, 2, 128, 128], P('blk', None, 'tp')
Inputs may be any that keep to these rules, and one draw needn't show every extreme that they name: `up_rows`: within each hidden column block, the 2 entries are distinct. `keep_mask`: bit k of word w holds the keep flag of hidden unit 16 w + k.
All inputs are finite; a program needn't handle non-finite values.
Results may differ from a plain program's by a relative error of at most 0.005.
Values may be sent and summed in bfloat16 or wider, within the bound.
No kernel may reach another device: no remote copies, remote signals or barrier semaphores. Data moves between devices by JAX's collectives and lax.ppermute only.
A program may use at most 64 MiB of HBM per device.

v0:
```python
import jax
import jax.numpy as jnp
from jax import lax
from jax.sharding import PartitionSpec as P

INV_ROOT_TWO = 0.7071067811865476
INV_ROOT_TAU = 0.3989422804014327
KEEP_SCALE = 1.25


def gelu_value(value):
    return 0.5 * value * (1.0 + jax.scipy.special.erf(value * INV_ROOT_TWO))


def gelu_slope(value):
    return (
        0.5 * (1.0 + jax.scipy.special.erf(value * INV_ROOT_TWO))
        + value * jnp.exp(-0.5 * value * value) * INV_ROOT_TAU
    )


def combine_terms(received, flat_owner, part_rows, row_blocks, tile):
    selector = (flat_owner[:, None] == jnp.arange(row_blocks, dtype=jnp.int32)[None, :]).astype(
        jnp.float32
    )
    stacked = received.reshape(part_rows, flat_owner.shape[0], tile)
    summed = jnp.einsum("nsl,sr->nrl", stacked, selector, precision=lax.Precision.HIGHEST)
    return summed.reshape(part_rows, row_blocks * tile).astype(jnp.bfloat16)


def per_device(inputs, grad_out, w_up, w_down, up_rows, slot_counts, keep_mask):
    tok_dev, width_local = inputs.shape
    col_local, slots, tile, _unused = w_up.shape
    parts = lax.axis_size("tp")
    blocks = lax.axis_size("blk")
    width = width_local * parts
    row_blocks = width // tile
    part_rows = tok_dev // parts
    held = part_rows * blocks
    span = col_local * slots
    live = jnp.arange(slots, dtype=jnp.int32)[None, :] < slot_counts[:, None]
    live_tiles = live[:, :, None, None]
    up_live = jnp.where(live_tiles, w_up, jnp.zeros((), jnp.bfloat16))
    down_live = jnp.where(live_tiles, w_down, jnp.zeros((), jnp.bfloat16))
    owner_rows = lax.all_gather(up_rows, "blk", axis=0, tiled=True)
    flat_owner = owner_rows.reshape(-1)

    def select_tiles(rows_full):
        blocked = rows_full.reshape(part_rows, row_blocks, tile)
        return jnp.take(blocked, flat_owner, axis=1).reshape(part_rows, blocks, span * tile)

    def as_tiles(received):
        return received.reshape(held, col_local, slots, tile)

    def combine(received):
        return combine_terms(received, flat_owner, part_rows, row_blocks, tile)

    in_rows, out_rows = (
        lax.all_to_all(inputs, "tp", split_axis=0, concat_axis=1, tiled=True),
        lax.all_to_all(grad_out, "tp", split_axis=0, concat_axis=1, tiled=True),
    )
    recv_in, recv_out = (
        lax.all_to_all(select_tiles(in_rows), "blk", split_axis=1, concat_axis=0, tiled=True),
        lax.all_to_all(select_tiles(out_rows), "blk", split_axis=1, concat_axis=0, tiled=True),
    )
    input_tiles = as_tiles(recv_in)
    cotangent_tiles = as_tiles(recv_out)
    word_count = keep_mask.shape[1]
    words = keep_mask.reshape(blocks, parts, part_rows, word_count)
    mine = lax.dynamic_index_in_dim(words, lax.axis_index("tp"), 1, keepdims=False).reshape(
        held, word_count
    )
    columns = jnp.arange(col_local * tile, dtype=jnp.int32)
    picked = jnp.take(mine, columns // 16, axis=1)
    keep = jnp.bitwise_and(jnp.right_shift(picked, columns % 16), 1)
    scale = keep.astype(jnp.float32) * KEEP_SCALE
    pre = jnp.einsum(
        "nckp,ckpj->ncj", input_tiles, up_live, preferred_element_type=jnp.float32
    ).reshape(held, col_local * tile)
    hidden = (gelu_value(pre) * scale).astype(jnp.bfloat16)
    hidden_blocks = hidden.reshape(held, col_local, tile)
    out_part = jnp.einsum(
        "ncj,ckjl->nckl", hidden_blocks, down_live, preferred_element_type=jnp.float32
    ).reshape(held, span * tile)
    grad_hidden = jnp.einsum(
        "nckl,ckjl->ncj", cotangent_tiles, down_live, preferred_element_type=jnp.float32
    ).reshape(held, col_local * tile)
    grad_pre = (grad_hidden * scale * gelu_slope(pre)).astype(jnp.bfloat16)
    grad_blocks = grad_pre.reshape(held, col_local, tile)
    in_part = jnp.einsum(
        "ncj,ckpj->nckp", grad_blocks, up_live, preferred_element_type=jnp.float32
    ).reshape(held, span * tile)
    out_recv, in_recv = (
        lax.all_to_all(out_part, "blk", split_axis=0, concat_axis=1, tiled=True),
        lax.all_to_all(in_part, "blk", split_axis=0, concat_axis=1, tiled=True),
    )
    outputs, grad_in = (
        lax.all_to_all(combine(out_recv), "tp", split_axis=1, concat_axis=0, tiled=True),
        lax.all_to_all(combine(in_recv), "tp", split_axis=1, concat_axis=0, tiled=True),
    )
    up_sum = jnp.einsum(
        "nckp,ncj->ckpj", input_tiles, grad_blocks, preferred_element_type=jnp.float32
    )
    down_sum = jnp.einsum(
        "ncj,nckl->ckjl", hidden_blocks, cotangent_tiles, preferred_element_type=jnp.float32
    )
    up_share, down_share = (
        lax.psum_scatter(up_sum, "tp", scatter_dimension=2, tiled=True),
        lax.psum_scatter(down_sum, "tp", scatter_dimension=2, tiled=True),
    )
    grad_up = jnp.where(live_tiles, up_share, 0.0).astype(jnp.bfloat16)
    grad_down = jnp.where(live_tiles, down_share, 0.0).astype(jnp.bfloat16)
    return (outputs, grad_in, grad_up, grad_down)


def solution(mesh):
    return jax.shard_map(
        per_device,
        mesh=mesh,
        in_specs=(
            P("blk", "tp"),
            P("blk", "tp"),
            P("blk", None, None, None),
            P("blk", None, None, None),
            P("blk", None),
            P("blk"),
            P(None, "blk"),
        ),
        out_specs=(
            P("blk", "tp"),
            P("blk", "tp"),
            P("blk", None, "tp", None),
            P("blk", None, "tp", None),
        ),
        check_vma=False,
    )
```

profile of v0, /device:TPU:10, one launch (start us, length us, event | category | flops | bytes accessed | tf_op | source)
XLA Modules:
  0.0 286.7 jit_solution(3485483218817559302)
XLA Ops:
  7.2 3.6 %all-to-all-start = ((bf16[2,64,4096]{2,1,0:T(8,128)(2,1)}), bf16[2,64,4096]{2,1,0:T(8,128)(2,1)S(1)}, u32[]{:S(2)}, u32[]{:S(2)}) async-start(bf16[2,64,4096]{2,1,0:T(8,128)(2,1)} %bitcast.103), calls=%async_computation | async-start | bytes 2097152 | tf_op jit(solution)/shard_map/all_to_all | solution.py:59
  10.8 15.2 %all-gather = s32[16,2,2]{2,1,0:T(2,128)S(1)} all-gather(s32[1,2,2]{2,1,0:T(2,128)S(1)} %bitcast.105), channel_id=1, replica_groups=mesh['blk'=16,'tp'=2] {'blk'}, dimensions={0}, use_global_device_ids=true | all-gather | bytes 272 | tf_op jit(solution)/shard_map/all_gather | solution.py:45
  26.1 3.6 %all-to-all-start.4 = ((bf16[2,64,4096]{2,1,0:T(8,128)(2,1)}), bf16[2,64,4096]{2,1,0:T(8,128)(2,1)S(1)}, u32[]{:S(2)}, u32[]{:S(2)}) async-start(bf16[2,64,4096]{2,1,0:T(8,128)(2,1)} %bitcast.20), calls=%async_computation.4 | async-start | bytes 2097152 | tf_op jit(solution)/shard_map/all_to_all | solution.py:60
  29.7 1.1 copy.51
  32.3 11.9 %all-to-all-done.4 = bf16[2,64,4096]{2,1,0:T(8,128)(2,1)S(1)} async-done(((bf16[2,64,4096]{2,1,0:T(8,128)(2,1)}), bf16[2,64,4096]{2,1,0:T(8,128)(2,1)S(1)}, u32[]{:S(2)}, u32[]{:S(2)}) %all-to-all-start.4) | async-done | bytes 1048608 | tf_op jit(solution)/shard_map/all_to_all | solution.py:60
  44.3 1.1 copy.63
  45.4 1.6 reshape.191
  47.0 1.9 copy.64
  52.0 1.5 copy.66
  53.6 10.4 %all-to-all-start.5 = ((bf16[64,16,512]{2,0,1:T(8,128)(2,1)}), bf16[64,16,512]{2,0,1:T(8,128)(2,1)S(1)}, u32[]{:S(2)}, u32[]{:S(2)}) async-start(bf16[64,16,512]{2,0,1:T(8,128)(2,1)} %copy.66), calls=%async_computation.5 | async-start | bytes 2097152 | tf_op jit(solution)/shard_map/all_to_all | solution.py:64
  65.3 1.5 copy.54
  66.9 21.7 %all-to-all-done.5 = bf16[64,16,512]{2,0,1:T(8,128)(2,1)S(1)} async-done(((bf16[64,16,512]{2,0,1:T(8,128)(2,1)}), bf16[64,16,512]{2,0,1:T(8,128)(2,1)S(1)}, u32[]{:S(2)}, u32[]{:S(2)}) %all-to-all-start.5) | async-done | bytes 1048608 | tf_op jit(solution)/shard_map/all_to_all | solution.py:64
  88.6 5.1 %all-to-all-start.1 = ((bf16[64,16,512]{2,0,1:T(8,128)(2,1)}), bf16[64,16,512]{2,0,1:T(8,128)(2,1)S(1)}, u32[]{:S(2)}, u32[]{:S(2)}) async-start(bf16[64,16,512]{2,0,1:T(8,128)(2,1)} %copy.54), calls=%async_computation.1 | async-start | bytes 2097152 | tf_op jit(solution)/shard_map/all_to_all | solution.py:63
  94.2 1.1 gather_fusion
  95.4 1.2 reshape.193
  96.6 3.7 %copy.74 = bf16[1024,2,2,128]{0,3,2,1:T(8,128)(2,1)} copy(bf16[1024,2,2,128]{3,2,1,0:T(2,128)(2,1)} %reshape.193) | data formatting | bytes 2097152 | tf_op jit(solution)/shard_map/reshape | solution.py:53
  100.3 17.9 %all-to-all-done.1 = bf16[64,16,512]{2,0,1:T(8,128)(2,1)S(1)} async-done(((bf16[64,16,512]{2,0,1:T(8,128)(2,1)}), bf16[64,16,512]{2,0,1:T(8,128)(2,1)S(1)}, u32[]{:S(2)}, u32[]{:S(2)}) %all-to-all-start.1) | async-done | bytes 1048608 | tf_op jit(solution)/shard_map/all_to_all | solution.py:63
  118.2 1.1 reshape.187
  119.3 2.5 copy.72
  124.7 1.8 convolution_bitcast_fusion
  126.6 3.1 %copy.69 = f32[1024,2,2,128]{3,2,1,0:T(2,128)S(1)} copy(f32[1024,2,2,128]{0,3,2,1:T(8,128)} %convolution_bitcast_fusion) | data formatting | bytes 4194304 | tf_op jit(solution)/shard_map/ncj,ckpj->nckp/transpose | solution.py:90
  129.7 2.7 all_to_all.112
  132.4 5.1 %all-to-all-start.6 = ((f32[16,64,512]{2,1,0:T(8,128)}), f32[16,64,512]{2,1,0:T(8,128)S(1)}, u32[]{:S(2)}, u32[]{:S(2)}) async-start(f32[16,64,512]{2,1,0:T(8,128)} %all_to_all.112), calls=%async_computation.6 | async-start | bytes 4194304 | tf_op jit(solution)/shard_map/all_to_all | solution.py:95
  137.5 2.0 fusion.10
  140.3 1.9 convolution_bitcast_fusion.1
  142.2 4.1 %copy.60 = f32[1024,2,2,128]{3,2,1,0:T(2,128)} copy(f32[1024,2,2,128]{0,3,2,1:T(8,128)} %convolution_bitcast_fusion.1) | data formatting | bytes 4194304 | tf_op jit(solution)/shard_map/ncj,ckjl->nckl/transpose | solution.py:82
  146.3 3.9 %all_to_all.100 = f32[16,64,512]{2,1,0:T(8,128)} reshape(f32[1024,2,2,128]{3,2,1,0:T(2,128)} %copy.60) | data formatting | bytes 4194304 | tf_op jit(solution)/shard_map/all_to_all | solution.py:94
  150.2 34.4 %all-to-all-done.6 = f32[16,64,512]{2,1,0:T(8,128)S(1)} async-done(((f32[16,64,512]{2,1,0:T(8,128)}), f32[16,64,512]{2,1,0:T(8,128)S(1)}, u32[]{:S(2)}, u32[]{:S(2)}) %all-to-all-start.6) | async-done | bytes 2097184 | tf_op jit(solution)/shard_map/all_to_all | solution.py:95
  184.6 1.3 copy-done
  185.9 5.1 %all-to-all-start.2 = ((f32[16,64,512]{2,1,0:T(8,128)}), f32[16,64,512]{2,1,0:T(8,128)S(1)}, u32[]{:S(2)}, u32[]{:S(2)}) async-start(f32[16,64,512]{2,1,0:T(8,128)} %all_to_all.100), calls=%async_computation.2 | async-start | bytes 4194304 | tf_op jit(solution)/shard_map/all_to_all | solution.py:94
  191.0 2.2 fusion.26
  193.3 4.2 %copy.70 = f32[64,16,512]{2,1,0:T(8,128)} copy(f32[64,16,512]{2,0,1:T(8,128)} %bitcast.95) | data formatting | bytes 4194304 | tf_op jit(solution)/shard_map/all_to_all | solution.py:95
  197.4 2.6 reshape.194
  200.1 2.8 fusion.1
  202.9 1.1 convert_element_type.49
  204.0 2.8 copy.71
  206.9 31.3 %all-to-all-done.2 = f32[16,64,512]{2,1,0:T(8,128)S(1)} async-done(((f32[16,64,512]{2,1,0:T(8,128)}), f32[16,64,512]{2,1,0:T(8,128)S(1)}, u32[]{:S(2)}, u32[]{:S(2)}) %all-to-all-start.2) | async-done | bytes 2097184 | tf_op jit(solution)/shard_map/all_to_all | solution.py:94
  238.1 4.4 %all-to-all-start.7 = ((bf16[64,2,4096]{2,0,1:T(8,128)(2,1)}), bf16[64,2,4096]{2,0,1:T(8,128)(2,1)}, u32[]{:S(2)}, u32[]{:S(2)}) async-start(bf16[64,2,4096]{2,0,1:T(8,128)(2,1)} %copy.71), calls=%async_computation.7 | async-start | bytes 2097152 | tf_op jit(solution)/shard_map/all_to_all | solution.py:99
  242.8 2.4 convolution_bitcast_fusion.4
  245.3 2.6 copy.61
  247.9 1.6 reshape.190
  249.5 1.3 fusion
  251.1 1.6 copy.62
  252.6 7.3 %all-to-all-done.7 = bf16[64,2,4096]{2,0,1:T(8,128)(2,1)} async-done(((bf16[64,2,4096]{2,0,1:T(8,128)(2,1)}), bf16[64,2,4096]{2,0,1:T(8,128)(2,1)}, u32[]{:S(2)}, u32[]{:S(2)}) %all-to-all-start.7) | async-done | bytes 1048608 | tf_op jit(solution)/shard_map/all_to_all | solution.py:99
  259.9 3.6 %all-to-all-start.3 = ((bf16[64,2,4096]{2,0,1:T(8,128)(2,1)}), bf16[64,2,4096]{2,0,1:T(8,128)(2,1)S(1)}, u32[]{:S(2)}, u32[]{:S(2)}) async-start(bf16[64,2,4096]{2,0,1:T(8,128)(2,1)} %copy.62), calls=%async_computation.3 | async-start | bytes 2097152 | tf_op jit(solution)/shard_map/all_to_all | solution.py:98
  263.5 1.7 select_convert_fusion
  265.3 11.3 %all-to-all-done.3 = bf16[64,2,4096]{2,0,1:T(8,128)(2,1)S(1)} async-done(((bf16[64,2,4096]{2,0,1:T(8,128)(2,1)}), bf16[64,2,4096]{2,0,1:T(8,128)(2,1)S(1)}, u32[]{:S(2)}, u32[]{:S(2)}) %all-to-all-start.3) | async-done | bytes 1048608 | tf_op jit(solution)/shard_map/all_to_all | solution.py:98
  277.6 2.3 copy.98
  (59 shorter events, 12.0 us)
Async XLA Ops:
  7.2 3.6 %copy-start.12 = (s32[2,2]{1,0:T(2,128)S(1)}, s32[2,2]{1,0:T(2,128)}, u32[]{:S(2)}) copy-start(s32[2,2]{1,0:T(2,128)} %param.13) | copy-start | bytes 52
  7.2 18.9 %all-to-all-start = ((bf16[2,64,4096]{2,1,0:T(8,128)(2,1)}), bf16[2,64,4096]{2,1,0:T(8,128)(2,1)S(1)}, u32[]{:S(2)}, u32[]{:S(2)}) async-start(bf16[2,64,4096]{2,1,0:T(8,128)(2,1)} %bitcast.103), calls=%async_computation | async-start | bytes 2097152 | tf_op jit(solution)/shard_map/all_to_all | solution.py:59
  26.1 18.2 %all-to-all-start.4 = ((bf16[2,64,4096]{2,1,0:T(8,128)(2,1)}), bf16[2,64,4096]{2,1,0:T(8,128)(2,1)S(1)}, u32[]{:S(2)}, u32[]{:S(2)}) async-start(bf16[2,64,4096]{2,1,0:T(8,128)(2,1)} %bitcast.20), calls=%async_computation.4 | async-start | bytes 2097152 | tf_op jit(solution)/shard_map/all_to_all | solution.py:60
  53.6 35.0 %all-to-all-start.5 = ((bf16[64,16,512]{2,0,1:T(8,128)(2,1)}), bf16[64,16,512]{2,0,1:T(8,128)(2,1)S(1)}, u32[]{:S(2)}, u32[]{:S(2)}) async-start(bf16[64,16,512]{2,0,1:T(8,128)(2,1)} %copy.66), calls=%async_computation.5 | async-start | bytes 2097152 | tf_op jit(solution)/shard_map/all_to_all | solution.py:64
  65.3 28.3 %copy-start.10 = (s32[2048,16]{0,1:T(8,128)S(1)}, s32[2048,16]{0,1:T(8,128)}, u32[]{:S(2)}) copy-start(s32[2048,16]{0,1:T(8,128)} %param.15) | copy-start | bytes 393220
  88.6 5.4 %copy-start.5 = (bf16[64,16,512]{2,0,1:T(8,128)(2,1)}, bf16[64,16,512]{2,0,1:T(8,128)(2,1)S(1)}, u32[]{:S(2)}) copy-start(bf16[64,16,512]{2,0,1:T(8,128)(2,1)S(1)} %all-to-all-done.5) | copy-start | bytes 3145732
  88.6 29.7 %all-to-all-start.1 = ((bf16[64,16,512]{2,0,1:T(8,128)(2,1)}), bf16[64,16,512]{2,0,1:T(8,128)(2,1)S(1)}, u32[]{:S(2)}, u32[]{:S(2)}) async-start(bf16[64,16,512]{2,0,1:T(8,128)(2,1)} %copy.54), calls=%async_computation.1 | async-start | bytes 2097152 | tf_op jit(solution)/shard_map/all_to_all | solution.py:63
  94.1 1.1 copy-start.13
  94.1 1.2 copy-start.6
  95.2 27.0 %copy-start.3 = (s32[256,1024]{1,0:T(8,128)}, s32[256,1024]{1,0:T(8,128)S(1)}, u32[]{:S(2)}) copy-start(s32[256,1024]{1,0:T(8,128)S(1)} %gather_fusion) | copy-start | bytes 3145732
  118.2 3.6 %copy-start.9 = (bf16[2,2,128,128]{3,2,1,0:T(8,128)(2,1)S(1)}, bf16[2,2,128,128]{3,2,1,0:T(8,128)(2,1)}, u32[]{:S(2)}) copy-start(bf16[2,2,128,128]{3,2,1,0:T(8,128)(2,1)} %param.11) | copy-start | bytes 393220
  119.3 3.0 %copy-start.11 = (bf16[2,2,128,128]{3,2,1,0:T(8,128)(2,1)S(1)}, bf16[2,2,128,128]{3,2,1,0:T(8,128)(2,1)}, u32[]{:S(2)}) copy-start(bf16[2,2,128,128]{3,2,1,0:T(8,128)(2,1)} %param.12) | copy-start | bytes 393220
  121.8 1.2 copy-start.4
  122.3 1.6 copy-start.7
  123.9 0.8 copy-start.8
  132.4 52.2 %all-to-all-start.6 = ((f32[16,64,512]{2,1,0:T(8,128)}), f32[16,64,512]{2,1,0:T(8,128)S(1)}, u32[]{:S(2)}, u32[]{:S(2)}) async-start(f32[16,64,512]{2,1,0:T(8,128)} %all_to_all.112), calls=%async_computation.6 | async-start | bytes 4194304 | tf_op jit(solution)/shard_map/all_to_all | solution.py:95
  139.4 0.8 copy-start.1
  184.6 1.3 copy-start
  185.9 52.2 %all-to-all-start.2 = ((f32[16,64,512]{2,1,0:T(8,128)}), f32[16,64,512]{2,1,0:T(8,128)S(1)}, u32[]{:S(2)}, u32[]{:S(2)}) async-start(f32[16,64,512]{2,1,0:T(8,128)} %all_to_all.100), calls=%async_computation.2 | async-start | bytes 4194304 | tf_op jit(solution)/shard_map/all_to_all | solution.py:94
  191.0 72.5 %reduce-scatter.3.cloned.1.call-start = ((), (), s32[]{:S(2)}) async-start(), calls=%async_computation.10 | async-start | bytes 393216 | tf_op jit(solution)/shard_map/reduce_scatter | solution.py:108
  204.0 38.8 %copy-start.2 = (bf16[1024,2,128,1]{0,2,3,1:T(8,128)(2,1)S(1)}, bf16[1024,2,128,1]{0,2,3,1:T(8,128)(2,1)}, u32[]{:S(2)}) copy-start(bf16[1024,2,128,1]{0,2,3,1:T(8,128)(2,1)} %copy-done.1) | copy-start | bytes 1572868
  238.1 21.8 %all-to-all-start.7 = ((bf16[64,2,4096]{2,0,1:T(8,128)(2,1)}), bf16[64,2,4096]{2,0,1:T(8,128)(2,1)}, u32[]{:S(2)}, u32[]{:S(2)}) async-start(bf16[64,2,4096]{2,0,1:T(8,128)(2,1)} %copy.71), calls=%async_computation.7 | async-start | bytes 2097152 | tf_op jit(solution)/shard_map/all_to_all | solution.py:99
  242.6 21.0 %reduce-scatter.5.cloned.1.call-start = ((), (), s32[]{:S(2)}) async-start(), calls=%async_computation.11 | async-start | bytes 393216 | tf_op jit(solution)/shard_map/reduce_scatter | solution.py:109
  259.9 16.7 %all-to-all-start.3 = ((bf16[64,2,4096]{2,0,1:T(8,128)(2,1)}), bf16[64,2,4096]{2,0,1:T(8,128)(2,1)S(1)}, u32[]{:S(2)}, u32[]{:S(2)}) async-start(bf16[64,2,4096]{2,0,1:T(8,128)(2,1)} %copy.62), calls=%async_computation.3 | async-start | bytes 2097152 | tf_op jit(solution)/shard_map/all_to_all | solution.py:98
Sparse Core Ops, SparseCore 0:
  194.0 11.7 reduce-scatter.2
  245.6 14.8 reduce-scatter.4
where the time goes:
time: 288 us; the launch traced here: 287 us
  waiting for transfers between devices  136 us (47%)
  local copies, waits for them, and re-layouts  62.2 us (22%)
  starting transfers between devices  41.1 us (14%)
  blocking collectives  15.2 us (5%)
  between operations  14.5 us (5%)
  matrix products  13.7 us (5%)
  other arithmetic  4.05 us (1%)
    all_to_all x1, waiting for transfers between devices, per_device(): lax.all_to_all(in_part, 'blk', split_axis=0, concat_axis=1, tiled=True)  34.4 us
    all_to_all x1, waiting for transfers between devices, per_device(): lax.all_to_all(out_part, 'blk', split_axis=0, concat_axis=1, tiled=True)  31.3 us
    all_to_all x1, waiting for transfers between devices, per_device(): lax.all_to_all(select_tiles(out_rows), 'blk', split_axis=1, concat_axis=0...  21.7 us
    all_to_all x1, waiting for transfers between devices, per_device(): lax.all_to_all(select_tiles(in_rows), 'blk', split_axis=1, concat_axis=0,...  17.9 us
    all_gather x1, blocking collectives, per_device(): owner_rows = lax.all_gather(up_rows, 'blk', axis=0, tiled=True)  15.2 us
    all_to_all x1, waiting for transfers between devices, per_device(): lax.all_to_all(grad_out, 'tp', split_axis=0, concat_axis=1, tiled=True)  11.9 us
    all_to_all x1, waiting for transfers between devices, per_device(): lax.all_to_all(combine(out_recv), 'tp', split_axis=1, concat_axis=0, tile...  11.3 us
    all_to_all x1, starting transfers between devices, per_device(): lax.all_to_all(select_tiles(out_rows), 'blk', split_axis=1, concat_axis=0...  10.4 us
  transfers between devices with their start and end apart: 10, of which 7 were waited for; matrix products, arithmetic and copies ran while one was open for 17% of the time, Pallas kernels for 0%

commit v1 on v0

--- a/solution.py
+++ b/solution.py
@@ -61,7 +61,15 @@
     )
     recv_in, recv_out = (
         lax.all_to_all(select_tiles(in_rows), "blk", split_axis=1, concat_axis=0, tiled=True),
-        lax.all_to_all(select_tiles(out_rows), "blk", split_axis=1, concat_axis=0, tiled=True),
+        jnp.concatenate(
+            lax.all_to_all(
+                jnp.stack(jnp.split(select_tiles(out_rows), lax.axis_size("blk"), axis=1)),
+                "blk",
+                0,
+                0,
+            ),
+            axis=0,
+        ),
     )
     input_tiles = as_tiles(recv_in)
     cotangent_tiles = as_tiles(recv_out)

time: 288 us -> 299 us (1.038)
  local copies, waits for them, and re-layouts: 62.2 us -> 72.8 us
    unnamed x30 -> x45, local copies, waits for them, and re-layouts: 7.06 us -> 16.7 us
    another operation x0 -> x3, local copies, waits for them, and re-layouts: none -> 5.53 us  [the longest x2 4.89 us: as_tiles(): return received.reshape(held, col_local, slots, tile)]
    reshape x4 -> x2, local copies, waits for them, and re-layouts: 8.48 us -> 3.58 us  [as_tiles(): return received.reshape(held, col_local, slots, tile)]
  transfers between devices with their start and end apart: 10 -> 10, of which waited for: 7 -> 7; matrix products, arithmetic and copies ran while one was open for 17% -> 16% of each run, Pallas kernels for 0% -> 0%
where the time goes in v1:
time: 299 us; the launch traced here: 297 us
  waiting for transfers between devices  136 us (45%)
  local copies, waits for them, and re-layouts  72.8 us (24%)
  starting transfers between devices  41.1 us (14%)
  blocking collectives  15.2 us (5%)
  between operations  14.5 us (5%)
  matrix products  13.7 us (5%)
  other arithmetic  4.05 us (1%)
    all_to_all x1, waiting for transfers between devices, per_device(): lax.all_to_all(in_part, 'blk', split_axis=0, concat_axis=1, tiled=True)  34.4 us
    all_to_all x1, waiting for transfers between devices, per_device(): lax.all_to_all(out_part, 'blk', split_axis=0, concat_axis=1, tiled=True)  31.3 us
    all_to_all x1, waiting for transfers between devices, per_device(): lax.all_to_all(jnp.stack(jnp.split(select_tiles(out_rows), lax.axis_size(...  21.7 us
    all_to_all x1, waiting for transfers between devices, per_device(): lax.all_to_all(select_tiles(in_rows), 'blk', split_axis=1, concat_axis=0,...  18 us
    unnamed x45, local copies, waits for them, and re-layouts  16.7 us
    all_gather x1, blocking collectives, per_device(): owner_rows = lax.all_gather(up_rows, 'blk', axis=0, tiled=True)  15.2 us
    all_to_all x1, waiting for transfers between devices, per_device(): lax.all_to_all(grad_out, 'tp', split_axis=0, concat_axis=1, tiled=True)  11.9 us
    all_to_all x1, waiting for transfers between devices, per_device(): lax.all_to_all(combine(out_recv), 'tp', split_axis=1, concat_axis=0, tile...  11.3 us
  transfers between devices with their start and end apart: 10, of which 7 were waited for; matrix products, arithmetic and copies ran while one was open for 16% of the time, Pallas kernels for 0%

profile of v1, /device:TPU:10, one launch (start us, length us, event | category | flops | bytes accessed | tf_op | source)
XLA Modules:
  0.0 297.2 jit_solution(13394984744151523534)
XLA Ops:
  7.2 3.6 %all-to-all-start = ((bf16[2,64,4096]{2,1,0:T(8,128)(2,1)}), bf16[2,64,4096]{2,1,0:T(8,128)(2,1)S(1)}, u32[]{:S(2)}, u32[]{:S(2)}) async-start(bf16[2,64,4096]{2,1,0:T(8,128)(2,1)} %bitcast.131), calls=%async_computation | async-start | bytes 2097152 | tf_op jit(solution)/shard_map/all_to_all | solution.py:59
  10.8 15.2 %all-gather = s32[16,2,2]{2,1,0:T(2,128)S(1)} all-gather(s32[1,2,2]{2,1,0:T(2,128)S(1)} %bitcast.133), channel_id=1, replica_groups=mesh['blk'=16,'tp'=2] {'blk'}, dimensions={0}, use_global_device_ids=true | all-gather | bytes 272 | tf_op jit(solution)/shard_map/all_gather | solution.py:45
  26.1 3.6 %all-to-all-start.4 = ((bf16[2,64,4096]{2,1,0:T(8,128)(2,1)}), bf16[2,64,4096]{2,1,0:T(8,128)(2,1)S(1)}, u32[]{:S(2)}, u32[]{:S(2)}) async-start(bf16[2,64,4096]{2,1,0:T(8,128)(2,1)} %bitcast.20), calls=%async_computation.4 | async-start | bytes 2097152 | tf_op jit(solution)/shard_map/all_to_all | solution.py:60
  29.8 1.1 copy.545
  32.4 11.9 %all-to-all-done.4 = bf16[2,64,4096]{2,1,0:T(8,128)(2,1)S(1)} async-done(((bf16[2,64,4096]{2,1,0:T(8,128)(2,1)}), bf16[2,64,4096]{2,1,0:T(8,128)(2,1)S(1)}, u32[]{:S(2)}, u32[]{:S(2)}) %all-to-all-start.4) | async-done | bytes 1048608 | tf_op jit(solution)/shard_map/all_to_all | solution.py:60
  44.3 1.1 copy.557
  45.4 1.6 reshape.187
  47.0 1.9 copy.558
  52.1 1.8 fusion.26
  64.1 10.4 %all-to-all-start.5 = ((bf16[16,64,1,512]{3,1,2,0:T(8,128)(2,1)}), bf16[16,64,1,512]{3,1,2,0:T(8,128)(2,1)S(1)}, u32[]{:S(2)}, u32[]{:S(2)}) async-start(bf16[16,64,1,512]{3,1,2,0:T(8,128)(2,1)} %bitcast_dynamic-update-slice_fusion), calls=%async_computation.5 | async-start | bytes 2097152 | tf_op jit(solution)/shard_map/all_to_all | solution.py:65
  75.9 1.5 copy.548
  77.4 21.7 %all-to-all-done.5 = bf16[16,64,1,512]{3,1,2,0:T(8,128)(2,1)S(1)} async-done(((bf16[16,64,1,512]{3,1,2,0:T(8,128)(2,1)}), bf16[16,64,1,512]{3,1,2,0:T(8,128)(2,1)S(1)}, u32[]{:S(2)}, u32[]{:S(2)}) %all-to-all-start.5) | async-done | bytes 1048608 | tf_op jit(solution)/shard_map/all_to_all | solution.py:65
  99.1 5.1 %all-to-all-start.1 = ((bf16[64,16,512]{2,0,1:T(8,128)(2,1)}), bf16[64,16,512]{2,0,1:T(8,128)(2,1)S(1)}, u32[]{:S(2)}, u32[]{:S(2)}) async-start(bf16[64,16,512]{2,0,1:T(8,128)(2,1)} %copy.548), calls=%async_computation.1 | async-start | bytes 2097152 | tf_op jit(solution)/shard_map/all_to_all | solution.py:63
  104.7 1.1 gather_fusion
  105.9 1.2 reshape_reshape.3
  107.1 3.7 %copy.567 = bf16[1024,2,2,128]{0,3,2,1:T(8,128)(2,1)} copy(bf16[1024,2,2,128]{3,2,1,0:T(2,128)(2,1)} %reshape_reshape.3) | data formatting | bytes 2097152 | tf_op jit(solution)/shard_map/reshape;reshape | solution.py:53
  110.8 18.0 %all-to-all-done.1 = bf16[64,16,512]{2,0,1:T(8,128)(2,1)S(1)} async-done(((bf16[64,16,512]{2,0,1:T(8,128)(2,1)}), bf16[64,16,512]{2,0,1:T(8,128)(2,1)S(1)}, u32[]{:S(2)}, u32[]{:S(2)}) %all-to-all-start.1) | async-done | bytes 1048608 | tf_op jit(solution)/shard_map/all_to_all | solution.py:63
  128.8 1.1 reshape.183
  129.9 2.5 copy.565
  135.3 1.8 convolution_bitcast_fusion
  137.1 3.1 %copy.562 = f32[1024,2,2,128]{3,2,1,0:T(2,128)S(1)} copy(f32[1024,2,2,128]{0,3,2,1:T(8,128)} %convolution_bitcast_fusion) | data formatting | bytes 4194304 | tf_op jit(solution)/shard_map/ncj,ckpj->nckp/transpose | solution.py:98
  140.2 2.7 all_to_all.102
  142.9 5.1 %all-to-all-start.6 = ((f32[16,64,512]{2,1,0:T(8,128)}), f32[16,64,512]{2,1,0:T(8,128)S(1)}, u32[]{:S(2)}, u32[]{:S(2)}) async-start(f32[16,64,512]{2,1,0:T(8,128)} %all_to_all.102), calls=%async_computation.6 | async-start | bytes 4194304 | tf_op jit(solution)/shard_map/all_to_all | solution.py:103
  148.0 2.0 fusion.10
  150.8 1.9 convolution_bitcast_fusion.1
  152.7 4.1 %copy.554 = f32[1024,2,2,128]{3,2,1,0:T(2,128)} copy(f32[1024,2,2,128]{0,3,2,1:T(8,128)} %convolution_bitcast_fusion.1) | data formatting | bytes 4194304 | tf_op jit(solution)/shard_map/ncj,ckjl->nckl/transpose | solution.py:90
  156.9 3.9 %all_to_all.92 = f32[16,64,512]{2,1,0:T(8,128)} reshape(f32[1024,2,2,128]{3,2,1,0:T(2,128)} %copy.554) | data formatting | bytes 4194304 | tf_op jit(solution)/shard_map/all_to_all | solution.py:102
  160.7 34.4 %all-to-all-done.6 = f32[16,64,512]{2,1,0:T(8,128)S(1)} async-done(((f32[16,64,512]{2,1,0:T(8,128)}), f32[16,64,512]{2,1,0:T(8,128)S(1)}, u32[]{:S(2)}, u32[]{:S(2)}) %all-to-all-start.6) | async-done | bytes 2097184 | tf_op jit(solution)/shard_map/all_to_all | solution.py:103
  195.2 1.3 copy-done
  196.5 5.1 %all-to-all-start.2 = ((f32[16,64,512]{2,1,0:T(8,128)}), f32[16,64,512]{2,1,0:T(8,128)S(1)}, u32[]{:S(2)}, u32[]{:S(2)}) async-start(f32[16,64,512]{2,1,0:T(8,128)} %all_to_all.92), calls=%async_computation.2 | async-start | bytes 4194304 | tf_op jit(solution)/shard_map/all_to_all | solution.py:102
  201.6 2.2 fusion.27
  203.8 4.2 %copy.563 = f32[64,16,512]{2,1,0:T(8,128)} copy(f32[64,16,512]{2,0,1:T(8,128)} %bitcast.124) | data formatting | bytes 4194304 | tf_op jit(solution)/shard_map/all_to_all | solution.py:103
  208.0 2.6 reshape.189
  210.6 2.8 fusion.1
  213.5 1.1 convert_element_type.49
  214.6 2.8 copy.564
  217.4 31.3 %all-to-all-done.2 = f32[16,64,512]{2,1,0:T(8,128)S(1)} async-done(((f32[16,64,512]{2,1,0:T(8,128)}), f32[16,64,512]{2,1,0:T(8,128)S(1)}, u32[]{:S(2)}, u32[]{:S(2)}) %all-to-all-start.2) | async-done | bytes 2097184 | tf_op jit(solution)/shard_map/all_to_all | solution.py:102
  248.7 4.4 %all-to-all-start.7 = ((bf16[64,2,4096]{2,0,1:T(8,128)(2,1)}), bf16[64,2,4096]{2,0,1:T(8,128)(2,1)}, u32[]{:S(2)}, u32[]{:S(2)}) async-start(bf16[64,2,4096]{2,0,1:T(8,128)(2,1)} %copy.564), calls=%async_computation.7 | async-start | bytes 2097152 | tf_op jit(solution)/shard_map/all_to_all | solution.py:107
  253.4 2.4 convolution_bitcast_fusion.4
  255.8 2.6 copy.555
  258.4 1.6 reshape.186
  260.0 1.3 fusion
  261.6 1.6 copy.556
  263.2 7.3 %all-to-all-done.7 = bf16[64,2,4096]{2,0,1:T(8,128)(2,1)} async-done(((bf16[64,2,4096]{2,0,1:T(8,128)(2,1)}), bf16[64,2,4096]{2,0,1:T(8,128)(2,1)}, u32[]{:S(2)}, u32[]{:S(2)}) %all-to-all-start.7) | async-done | bytes 1048608 | tf_op jit(solution)/shard_map/all_to_all | solution.py:107
  270.4 3.6 %all-to-all-start.3 = ((bf16[64,2,4096]{2,0,1:T(8,128)(2,1)}), bf16[64,2,4096]{2,0,1:T(8,128)(2,1)S(1)}, u32[]{:S(2)}, u32[]{:S(2)}) async-start(bf16[64,2,4096]{2,0,1:T(8,128)(2,1)} %copy.556), calls=%async_computation.3 | async-start | bytes 2097152 | tf_op jit(solution)/shard_map/all_to_all | solution.py:106
  274.1 1.7 select_convert_fusion
  275.8 11.3 %all-to-all-done.3 = bf16[64,2,4096]{2,0,1:T(8,128)(2,1)S(1)} async-done(((bf16[64,2,4096]{2,0,1:T(8,128)(2,1)}), bf16[64,2,4096]{2,0,1:T(8,128)(2,1)S(1)}, u32[]{:S(2)}, u32[]{:S(2)}) %all-to-all-start.3) | async-done | bytes 1048608 | tf_op jit(solution)/shard_map/all_to_all | solution.py:106
  288.1 2.3 copy.638
  (74 shorter events, 22.2 us)
Async XLA Ops:
  7.2 3.6 %copy-start.12 = (s32[2,2]{1,0:T(2,128)S(1)}, s32[2,2]{1,0:T(2,128)}, u32[]{:S(2)}) copy-start(s32[2,2]{1,0:T(2,128)} %param.13) | copy-start | bytes 52
  7.2 18.9 %all-to-all-start = ((bf16[2,64,4096]{2,1,0:T(8,128)(2,1)}), bf16[2,64,4096]{2,1,0:T(8,128)(2,1)S(1)}, u32[]{:S(2)}, u32[]{:S(2)}) async-start(bf16[2,64,4096]{2,1,0:T(8,128)(2,1)} %bitcast.131), calls=%async_computation | async-start | bytes 2097152 | tf_op jit(solution)/shard_map/all_to_all | solution.py:59
  26.1 18.2 %all-to-all-start.4 = ((bf16[2,64,4096]{2,1,0:T(8,128)(2,1)}), bf16[2,64,4096]{2,1,0:T(8,128)(2,1)S(1)}, u32[]{:S(2)}, u32[]{:S(2)}) async-start(bf16[2,64,4096]{2,1,0:T(8,128)(2,1)} %bitcast.20), calls=%async_computation.4 | async-start | bytes 2097152 | tf_op jit(solution)/shard_map/all_to_all | solution.py:60
  64.1 35.0 %all-to-all-start.5 = ((bf16[16,64,1,512]{3,1,2,0:T(8,128)(2,1)}), bf16[16,64,1,512]{3,1,2,0:T(8,128)(2,1)S(1)}, u32[]{:S(2)}, u32[]{:S(2)}) async-start(bf16[16,64,1,512]{3,1,2,0:T(8,128)(2,1)} %bitcast_dynamic-update-slice_fusion), calls=%async_computation.5 | async-start | bytes 2097152 | tf_op jit(solution)/shard_map/all_to_all | solution.py:65
  75.9 28.3 %copy-start.10 = (s32[2048,16]{0,1:T(8,128)S(1)}, s32[2048,16]{0,1:T(8,128)}, u32[]{:S(2)}) copy-start(s32[2048,16]{0,1:T(8,128)} %param.15) | copy-start | bytes 393220
  99.1 5.4 %copy-start.5 = (bf16[16,64,1,512]{3,1,2,0:T(8,128)(2,1)}, bf16[16,64,1,512]{3,1,2,0:T(8,128)(2,1)S(1)}, u32[]{:S(2)}) copy-start(bf16[16,64,1,512]{3,1,2,0:T(8,128)(2,1)S(1)} %all-to-all-done.5) | copy-start | bytes 3145732
  99.1 29.7 %all-to-all-start.1 = ((bf16[64,16,512]{2,0,1:T(8,128)(2,1)}), bf16[64,16,512]{2,0,1:T(8,128)(2,1)S(1)}, u32[]{:S(2)}, u32[]{:S(2)}) async-start(bf16[64,16,512]{2,0,1:T(8,128)(2,1)} %copy.548), calls=%async_computation.1 | async-start | bytes 2097152 | tf_op jit(solution)/shard_map/all_to_all | solution.py:63
  104.7 1.1 copy-start.13
  104.7 1.2 copy-start.6
  105.7 27.1 %copy-start.3 = (s32[256,1024]{1,0:T(8,128)}, s32[256,1024]{1,0:T(8,128)S(1)}, u32[]{:S(2)}) copy-start(s32[256,1024]{1,0:T(8,128)S(1)} %gather_fusion) | copy-start | bytes 3145732
  128.8 3.6 %copy-start.9 = (bf16[2,2,128,128]{3,2,1,0:T(8,128)(2,1)S(1)}, bf16[2,2,128,128]{3,2,1,0:T(8,128)(2,1)}, u32[]{:S(2)}) copy-start(bf16[2,2,128,128]{3,2,1,0:T(8,128)(2,1)} %param.11) | copy-start | bytes 393220
  129.9 3.0 copy-start.11
  132.4 1.2 copy-start.4
  132.8 1.6 copy-start.7
  134.4 0.8 copy-start.8
  142.9 52.2 %all-to-all-start.6 = ((f32[16,64,512]{2,1,0:T(8,128)}), f32[16,64,512]{2,1,0:T(8,128)S(1)}, u32[]{:S(2)}, u32[]{:S(2)}) async-start(f32[16,64,512]{2,1,0:T(8,128)} %all_to_all.102), calls=%async_computation.6 | async-start | bytes 4194304 | tf_op jit(solution)/shard_map/all_to_all | solution.py:103
  150.0 0.8 copy-start.1
  195.2 1.3 copy-start
  196.5 52.2 %all-to-all-start.2 = ((f32[16,64,512]{2,1,0:T(8,128)}), f32[16,64,512]{2,1,0:T(8,128)S(1)}, u32[]{:S(2)}, u32[]{:S(2)}) async-start(f32[16,64,512]{2,1,0:T(8,128)} %all_to_all.92), calls=%async_computation.2 | async-start | bytes 4194304 | tf_op jit(solution)/shard_map/all_to_all | solution.py:102
  201.5 72.5 %reduce-scatter.3.cloned.1.call-start = ((), (), s32[]{:S(2)}) async-start(), calls=%async_computation.10 | async-start | bytes 393216 | tf_op jit(solution)/shard_map/reduce_scatter | solution.py:116
  214.6 38.8 %copy-start.2 = (bf16[1024,2,128,1]{0,2,3,1:T(8,128)(2,1)S(1)}, bf16[1024,2,128,1]{0,2,3,1:T(8,128)(2,1)}, u32[]{:S(2)}) copy-start(bf16[1024,2,128,1]{0,2,3,1:T(8,128)(2,1)} %copy-done.1) | copy-start | bytes 1572868
  248.7 21.8 %all-to-all-start.7 = ((bf16[64,2,4096]{2,0,1:T(8,128)(2,1)}), bf16[64,2,4096]{2,0,1:T(8,128)(2,1)}, u32[]{:S(2)}, u32[]{:S(2)}) async-start(bf16[64,2,4096]{2,0,1:T(8,128)(2,1)} %copy.564), calls=%async_computation.7 | async-start | bytes 2097152 | tf_op jit(solution)/shard_map/all_to_all | solution.py:107
  253.1 21.0 %reduce-scatter.5.cloned.1.call-start = ((), (), s32[]{:S(2)}) async-start(), calls=%async_computation.11 | async-start | bytes 393216 | tf_op jit(solution)/shard_map/reduce_scatter | solution.py:117
  270.4 16.7 %all-to-all-start.3 = ((bf16[64,2,4096]{2,0,1:T(8,128)(2,1)}), bf16[64,2,4096]{2,0,1:T(8,128)(2,1)S(1)}, u32[]{:S(2)}, u32[]{:S(2)}) async-start(bf16[64,2,4096]{2,0,1:T(8,128)(2,1)} %copy.556), calls=%async_computation.3 | async-start | bytes 2097152 | tf_op jit(solution)/shard_map/all_to_all | solution.py:106
Sparse Core Ops, SparseCore 0:
  204.6 11.7 reduce-scatter.2
  256.2 14.8 reduce-scatter.4
